TPU v7x, 128 devices: a whole 4x4x4 slice. The times are simulated.
128 devices in a mesh: wide: 32 (over z, y, core), narrow: 4 (over x).
Axes of the slice: x: 4, y: 4, z: 4, core: 2. Of those that a mesh axis runs over, the one named last changes fastest.
Arguments:
- frames: float32 [131072, 440], P(('wide', 'narrow')), may hold values from -8 to 8
- targets: float32 [131072, 2048], P(('wide', 'narrow')), may hold values from -7 to 7
- projection: float32 [128, 440, 512], P(('wide', 'narrow')), may hold values from -0.25 to 0.25
- phases: float32 [128, 512], P(('wide', 'narrow')), may hold values from 0 to 6.283185
- block_order: int32 [128], replicated, may hold values from 0 to 127, each once
Outputs:
- residual: float32 [131072, 2048], P(('wide', 'narrow'))
- weights: float32 [2, 512, 2048], replicated
Inputs may be any that keep to these rules, and one draw needn't show every extreme that they name: `block_order`: a permutation; steps use its first 2 entries.
All inputs are finite; a program needn't handle non-finite values.
Results may differ from a plain program's by a relative error of at most 0.0003.
Values sent between devices are 32-bit elements; how exact they have to be, the bound alone decides.
A program may use at most 128 MiB of HBM per device.

v0:
```python
import jax
import jax.numpy as jnp
from jax import lax
from jax.sharding import PartitionSpec as P

STEPS = 2


def from_root(value, axis, source):
    kept = jnp.where(lax.axis_index(axis) == source, value, 0).astype(value.dtype)
    return lax.psum(kept, axis)


def features_of(frames, block_proj, block_phase):
    inner = jnp.dot(
        frames, block_proj, precision=lax.Precision.HIGHEST, preferred_element_type=jnp.float32
    )
    return jnp.sqrt(2.0 / block_proj.shape[1]) * jnp.cos(inner + block_phase[None, :])


def local_product(left, right):
    return jnp.dot(
        left.T, right, precision=lax.Precision.HIGHEST, preferred_element_type=jnp.float32
    )


def solve_block(gram_sum, cross_sum):
    width = gram_sum.shape[0]
    damping = 0.1 * jnp.trace(gram_sum) / width
    factor = jnp.linalg.cholesky(gram_sum + damping * jnp.eye(width, dtype=gram_sum.dtype))
    return jax.scipy.linalg.cho_solve((factor, True), cross_sum)


def per_device(frames, targets, projection, phases, block_order):
    feature_list = []
    for step_index in range(STEPS):
        block_proj, block_phase = (
            from_root(projection, ("wide", "narrow"), block_order[step_index]),
            from_root(phases, ("wide", "narrow"), block_order[step_index]),
        )
        feature_list.append(features_of(frames, block_proj[0], block_phase[0]))
    grams_local = jnp.stack([local_product(feats, feats) for feats in feature_list])
    grams_all = lax.psum(grams_local, ("wide", "narrow"))
    residual = targets
    solved = []
    for step_index in range(STEPS):
        feats = feature_list[step_index]
        cross_local = local_product(feats, residual)
        gram_sum = grams_all[step_index]
        cross_sum = lax.psum(cross_local, ("wide", "narrow"))
        weights = solve_block(gram_sum, cross_sum)
        residual = residual - jnp.dot(
            feats, weights, precision=lax.Precision.HIGHEST, preferred_element_type=jnp.float32
        )
        solved.append(weights)
    return (residual, jnp.stack(solved))


def solution(mesh):
    return jax.shard_map(
        per_device,
        mesh=mesh,
        in_specs=(
            P(("wide", "narrow"), None),
            P(("wide", "narrow"), None),
            P(("wide", "narrow"), None, None),
            P(("wide", "narrow"), None),
            P(),
        ),
        out_specs=(P(("wide", "narrow"), None), P()),
        check_vma=False,
    )
```

profile of v0, /device:TPU:1, one launch (start us, length us, event | category | flops | bytes accessed | tf_op | source)
XLA Modules:
  0.0 860.8 jit_solution(9181122696572727834)
XLA Ops:
  12.6 69.1 %all-reduce.1 = (f32[512]{0:T(512)S(1)}, f32[512]{0:T(512)S(1)}) all-reduce(f32[512]{0:T(512)S(1)} %bitcast.163, f32[512]{0:T(512)S(1)} %bitcast.162), channel_id=1, replica_groups=mesh['wide'=32,'narrow'=4] {'wide','narrow'}, use_global_device_ids=true, to_apply=%region_1.2 | all-reduce | flops 1024 | bytes 8192 | tf_op jit(solution)/shard_map/psum | solution.py:11
  81.7 85.6 %all-reduce.12.cloned.1.call-done = (f32[440,512]{1,0:T(8,128)}, f32[440,512]{1,0:T(8,128)}) async-done(((f32[440,512]{1,0:T(8,128)}, f32[440,512]{1,0:T(8,128)}), (f32[440,512]{1,0:T(8,128)}, f32[440,512]{1,0:T(8,128)})) %all-reduce.12.cloned.1.call-update) | async-done | bytes 1802256 | tf_op jit(solution)/shard_map/psum | solution.py:11
  167.3 11.2 %cosine_multiply_fusion.1 = f32[512,1024]{1,0:T(8,128)S(1)} fusion(f32[440,512]{1,0:T(8,128)} %get-tuple-element.42, f32[1024,440]{0,1:T(8,128)S(1)} %copy-done, f32[512]{0:T(512)S(1)} %get-tuple-element.38), kind=kOutput, calls=%fused_computation.61 | convolution fusion | flops 2769289216 | bytes 4802560 | tf_op jit(solution)/shard_map/dot_general | solution.py:15
  178.6 3.8 convolution_bitcast_fusion.1
  182.4 10.3 %cosine_multiply_fusion = f32[512,1024]{1,0:T(8,128)S(1)} fusion(f32[440,512]{1,0:T(8,128)S(1)} %copy-done.17, f32[1024,440]{0,1:T(8,128)S(1)} %copy-done, f32[512]{0:T(512)S(1)} %get-tuple-element.39), kind=kOutput, calls=%fused_computation.60 | convolution fusion | flops 2769289216 | bytes 4802560 | tf_op jit(solution)/shard_map/dot_general | solution.py:15
  197.7 15.2 %fusion.117 = f32[512,2048]{1,0:T(8,128)} fusion(f32[512,1024]{1,0:T(8,128)S(1)} %cosine_multiply_fusion.1, f32[1024,2048]{1,0:T(8,128)S(1)} %bitcast.159), kind=kOutput, calls=%fused_computation.198 | convolution fusion | flops 12884901888 | bytes 14680064 | tf_op jit(solution)/shard_map/dot_general | solution.py:22
  214.9 156.2 %all-reduce.10.cloned.1.call-done = (f32[512,2048]{1,0:T(8,128)}, f32[2,512,512]{1,2,0:T(8,128)}) async-done(((f32[512,2048]{1,0:T(8,128)}, f32[2,512,512]{1,2,0:T(8,128)}), (f32[512,2048]{1,0:T(8,128)}, f32[2,512,512]{1,2,0:T(8,128)})) %all-reduce.10.cloned.1.call-update) | async-done | bytes 6291472 | tf_op jit(solution)/shard_map/psum | solution.py:50
  381.9 11.7 %cholesky.358 = f32[128,128]{1,0:T(8,128)S(1)} custom-call(f32[128,128]{1,0:T(8,128)S(1)} %cholesky.439), custom_call_target="Cholesky" | custom-call | tf_op jit(solution)/shard_map/jit(cholesky)/cholesky | solution.py:30
  394.4 11.7 %cholesky.286 = f32[128,128]{1,0:T(8,128)S(1)} custom-call(f32[128,128]{1,0:T(8,128)S(1)} %cholesky.426), custom_call_target="Cholesky" | custom-call | tf_op jit(solution)/shard_map/jit(cholesky)/cholesky | solution.py:30
  406.9 9.8 %custom-call.29 = f32[1,128,128]{1,2,0:T(8,128)S(1)} custom-call(f32[1,128,128]{2,1,0:T(8,128)S(1)} %get-tuple-element.71), custom_call_target="InvertDiagBlocksLowerTriangular" | custom-call | tf_op jit(solution)/shard_map/jit(cholesky)/cholesky | solution.py:30
  417.4 10.0 %custom-call.33 = f32[1,128,128]{1,2,0:T(8,128)S(1)} custom-call(f32[1,128,128]{2,1,0:T(8,128)S(1)} %get-tuple-element.61), custom_call_target="InvertDiagBlocksLowerTriangular" | custom-call | tf_op jit(solution)/shard_map/jit(cholesky)/cholesky | solution.py:30
  430.0 11.7 %cholesky.377 = f32[128,128]{1,0:T(8,128)S(1)} custom-call(f32[128,128]{1,0:T(8,128)S(1)} %cholesky.443), custom_call_target="Cholesky" | custom-call | tf_op jit(solution)/shard_map/jit(cholesky)/cholesky | solution.py:30
  442.4 9.8 %custom-call.34 = f32[1,128,128]{1,2,0:T(8,128)S(1)} custom-call(f32[1,128,128]{2,1,0:T(8,128)S(1)} %get-tuple-element.58), custom_call_target="InvertDiagBlocksLowerTriangular" | custom-call | tf_op jit(solution)/shard_map/jit(cholesky)/cholesky | solution.py:30
  453.8 11.9 %cholesky.398 = f32[128,128]{1,0:T(8,128)S(1)} custom-call(f32[128,128]{1,0:T(8,128)S(1)} %cholesky.448), custom_call_target="Cholesky" | custom-call | tf_op jit(solution)/shard_map/jit(cholesky)/cholesky | solution.py:30
  465.7 9.8 %custom-call.35 = f32[1,128,128]{1,2,0:T(8,128)S(1)} custom-call(f32[1,128,128]{2,1,0:T(8,128)S(1)} %get-tuple-element.55), custom_call_target="InvertDiagBlocksLowerTriangular" | custom-call | tf_op jit(solution)/shard_map/jit(cholesky)/cholesky | solution.py:30
  477.0 11.7 %cholesky.415 = f32[128,128]{1,0:T(8,128)S(1)} custom-call(f32[128,128]{1,0:T(8,128)S(1)} %convolution_subtract_fusion.14), custom_call_target="Cholesky" | custom-call | tf_op jit(solution)/shard_map/jit(cholesky)/cholesky | solution.py:30
  489.6 11.7 %cholesky.305 = f32[128,128]{1,0:T(8,128)S(1)} custom-call(f32[128,128]{1,0:T(8,128)S(1)} %cholesky.430), custom_call_target="Cholesky" | custom-call | tf_op jit(solution)/shard_map/jit(cholesky)/cholesky | solution.py:30
  501.9 10.2 %custom-call.30 = f32[1,128,128]{1,2,0:T(8,128)S(1)} custom-call(f32[1,128,128]{2,1,0:T(8,128)S(1)} %get-tuple-element.68), custom_call_target="InvertDiagBlocksLowerTriangular" | custom-call | tf_op jit(solution)/shard_map/jit(cholesky)/cholesky | solution.py:30
  512.9 11.7 %cholesky.326 = f32[128,128]{1,0:T(8,128)S(1)} custom-call(f32[128,128]{1,0:T(8,128)S(1)} %cholesky.435), custom_call_target="Cholesky" | custom-call | tf_op jit(solution)/shard_map/jit(cholesky)/cholesky | solution.py:30
  525.3 9.8 %custom-call.31 = f32[1,128,128]{1,2,0:T(8,128)S(1)} custom-call(f32[1,128,128]{2,1,0:T(8,128)S(1)} %get-tuple-element.65), custom_call_target="InvertDiagBlocksLowerTriangular" | custom-call | tf_op jit(solution)/shard_map/jit(cholesky)/cholesky | solution.py:30
  535.7 11.9 %cholesky.343 = f32[128,128]{1,0:T(8,128)S(1)} custom-call(f32[128,128]{1,0:T(8,128)S(1)} %convolution_subtract_fusion.15), custom_call_target="Cholesky" | custom-call | tf_op jit(solution)/shard_map/jit(cholesky)/cholesky | solution.py:30
  551.0 8.3 while.4
  559.4 39.3 %custom-call.32 = f32[4,128,128]{1,2,0:T(8,128)S(1)} custom-call(f32[4,128,128]{2,1,0:T(8,128)S(1)} %get-tuple-element.18), custom_call_target="InvertDiagBlocksLowerTriangular" | custom-call | tf_op jit(solution)/shard_map/jit(_cho_solve)/triangular_solve | solution.py:31
  617.7 3.6 fusion.30
  623.3 16.1 %convolution_subtract_fusion.1 = f32[1024,2048]{1,0:T(8,128)S(1)} fusion(f32[1024,2048]{1,0:T(8,128)S(1)} %bitcast.161, f32[512,1024]{1,0:T(8,128)S(1)} %copy-done.6, f32[128,2048]{1,0:T(8,128)S(1)} %fusion.95, f32[128,2048]{1,0:T(8,128)} %copy-done.7, f32[128,2048]{1,0:T(8,128)} %copy-done.9, f32[128,2048]{1,0:T(8,128)} %fusion.90), kind=kOutput, calls=%fused_computation.8 | convolution fusion | flops 12890144768 | bytes 23068672 | tf_op jit(solution)/shard_map/dot_general | solution.py:52
  642.8 15.6 %fusion.118 = f32[512,2048]{1,0:T(8,128)} fusion(f32[512,1024]{1,0:T(8,128)S(1)} %copy-done.4, f32[1024,2048]{1,0:T(8,128)S(1)} %convolution_subtract_fusion.1), kind=kOutput, calls=%fused_computation.199 | convolution fusion | flops 12884901888 | bytes 14680064 | tf_op jit(solution)/shard_map/dot_general | solution.py:22
  664.6 11.9 %while.5 = (s32[]{:T(128)}, f32[512,512]{1,0:T(8,128)}, s32[4,2]{0,1:T(2,128)S(1)}, f32[4,128,128]{2,1,0:T(8,128)S(1)}, s32[]{:T(128)}) while((s32[]{:T(128)}, f32[512,512]{1,0:T(8,128)}, s32[4,2]{0,1:T(2,128)S(1)}, f32[4,128,128]{2,1,0:T(8,128)S(1)}, s32[]{:T(128)}) %tuple.74), condition=%wide.while_cond.clone, body=%wide.while_body.clone.sunk | while | flops 2 | bytes 131189 | solution.py:31
  677.2 40.3 %custom-call.36 = f32[4,128,128]{1,2,0:T(8,128)S(1)} custom-call(f32[4,128,128]{2,1,0:T(8,128)} %copy-done.18), custom_call_target="InvertDiagBlocksLowerTriangular" | custom-call | tf_op jit(solution)/shard_map/jit(_cho_solve)/triangular_solve | solution.py:31
  717.5 4.2 fusion.37
  721.7 89.9 %all-reduce.8.cloned.1.call-done = f32[512,2048]{1,0:T(8,128)} async-done(((f32[512,2048]{1,0:T(8,128)}), f32[512,2048]{1,0:T(8,128)}) %all-reduce.8.cloned.1.call-update) | async-done | bytes 4194320 | tf_op jit(solution)/shard_map/psum | solution.py:50
  831.7 16.0 %convolution_subtract_fusion = f32[1024,2048]{1,0:T(8,128)} fusion(f32[1024,2048]{1,0:T(8,128)S(1)} %bitcast.157, f32[512,1024]{1,0:T(8,128)S(1)} %copy-done.4, f32[128,2048]{1,0:T(8,128)S(1)} %fusion.102, f32[128,2048]{1,0:T(8,128)S(1)} %fusion.100, f32[128,2048]{1,0:T(8,128)S(1)} %fusion.98, f32[128,2048]{1,0:T(8,128)S(1)} %fusion.97), kind=kOutput, calls=%fused_computation.7 | convolution fusion | flops 12890144768 | bytes 23068672 | tf_op jit(solution)/shard_map/dot_general | solution.py:52
  849.9 4.0 pad_maximum_fusion
  (165 shorter events, 104.0 us)
Async XLA Ops:
  7.2 160.2 %copy-start = (f32[1024,440]{0,1:T(8,128)S(1)}, f32[1024,440]{0,1:T(8,128)}, u32[]{:S(2)}) copy-start(f32[1024,440]{0,1:T(8,128)} %param.8) | copy-start | bytes 5406724
  7.2 5.4 copy-start.19
  7.2 160.1 %all-reduce.12.cloned.1.call-start = ((), (), s32[]{:S(2)}) async-start(), calls=%async_computation.2 | async-start | bytes 3604480 | tf_op jit(solution)/shard_map/psum | solution.py:11
  12.6 358.6 %all-reduce.10.cloned.1.call-start = ((), (), s32[]{:S(2)}) async-start(), calls=%async_computation.1 | async-start | bytes 12582912 | tf_op jit(solution)/shard_map/psum | solution.py:50
  178.6 19.1 %copy-start.5 = (f32[512,1024]{1,0:T(8,128)}, f32[512,1024]{1,0:T(8,128)S(1)}, u32[]{:S(2)}) copy-start(f32[512,1024]{1,0:T(8,128)S(1)} %cosine_multiply_fusion.1) | copy-start | bytes 6291460
  178.6 3.8 copy-start.17
  178.6 19.0 %slice-start.2 = ((s8[8388608]{0:T(1024)(128)(4,1)}), s8[4194304]{0:T(1024)(128)(4,1)S(1)}, s32[]{:S(2)}) async-start(s8[8388608]{0:T(1024)(128)(4,1)} %bitcast.158), calls=%async_computation.5 | async-start | bytes 8388608
  182.4 15.3 %slice-start.3 = ((s8[8388608]{0:T(1024)(128)(4,1)}), s8[4194304]{0:T(1024)(128)(4,1)S(1)}, s32[]{:S(2)}) async-start(s8[8388608]{0:T(1024)(128)(4,1)} %bitcast.158), calls=%async_computation.6 | async-start | bytes 8388608
  192.7 1.3 copy-start.3
  214.4 597.3 %all-reduce.8.cloned.1.call-start = ((), (), s32[]{:S(2)}) async-start(), calls=%async_computation | async-start | bytes 8388608 | tf_op jit(solution)/shard_map/psum | solution.py:50
  380.8 1.0 copy-start.16
  381.9 107.0 %copy-start.15 = (f32[512,512]{1,0:T(8,128)S(1)}, f32[512,512]{1,0:T(8,128)}, u32[]{:S(2)}) copy-start(f32[512,512]{1,0:T(8,128)} %get-tuple-element.81) | copy-start | bytes 3145732
  488.7 62.2 %copy-start.10 = (f32[512,512]{1,0:T(8,128)}, f32[512,512]{1,0:T(8,128)S(1)}, u32[]{:S(2)}) copy-start(f32[512,512]{1,0:T(8,128)S(1)} %get-tuple-element.53) | copy-start | bytes 3145732
  559.4 47.4 %copy-start.12 = (f32[512,512]{1,0:T(8,128)}, f32[512,512]{1,0:T(8,128)S(1)}, u32[]{:S(2)}) copy-start(f32[512,512]{1,0:T(8,128)S(1)} %get-tuple-element.187) | copy-start | bytes 3145732
  601.0 3.5 copy-start.13
  610.9 12.3 %slice-start.4 = ((s8[8388608]{0:T(1024)(128)(4,1)}), s8[4194304]{0:T(1024)(128)(4,1)S(1)}, s32[]{:S(2)}) async-start(s8[8388608]{0:T(1024)(128)(4,1)} %bitcast.160), calls=%async_computation.7 | async-start | bytes 8388608
  614.0 7.2 copy-start.7
  616.6 6.7 slice-start.5
  617.6 3.7 copy-start.9
  617.7 5.6 copy-start.6
  623.3 19.5 %copy-start.4 = (f32[512,1024]{1,0:T(8,128)S(1)}, f32[512,1024]{1,0:T(8,128)}, u32[]{:S(2)}) copy-start(f32[512,1024]{1,0:T(8,128)} %copy-done.3) | copy-start | bytes 6291460
  639.4 3.4 copy-start.2
  676.5 0.7 copy-start.18
  813.9 3.5 copy-start.11
  814.0 3.5 copy-start.14
  825.0 6.7 slice-start
  827.5 4.1 slice-start.1
  847.7 2.2 copy-start.8
  849.9 4.0 copy-start.1
Sparse Core Ops, SparseCore 0:
  13.6 153.6 all-reduce.11
  214.5 156.5 all-reduce.9
  658.6 153.0 all-reduce.7
where the time goes:
time: 871 us; the launch traced here: 861 us
  waiting for transfers between devices  332 us (38%)
  other arithmetic  261 us (30%)
  matrix products  143 us (16%)
  blocking collectives  69.1 us (8%)
  local copies, waits for them, and re-layouts  32.4 us (4%)
  between operations  22.6 us (3%)
    psum x2, waiting for transfers between devices, per_device(): cross_sum = lax.psum(cross_local, ('wide', 'narrow'))  246 us
    another operation x30, other arithmetic, solve_block(): jnp.linalg.cholesky(gram_sum + damping * jnp.eye(width, dtype=gram_sum.dt...  159 us
    psum x1, waiting for transfers between devices, from_root(): return lax.psum(kept, axis)  85.6 us
    another operation x5, other arithmetic, solve_block(): return jax.scipy.linalg.cho_solve((factor, True), cross_sum)  82.1 us
    psum x1, blocking collectives, from_root(): return lax.psum(kept, axis)  69.1 us
    another operation x28, matrix products, solve_block(): return jax.scipy.linalg.cho_solve((factor, True), cross_sum)  44.2 us
    dot_general x4, matrix products, local_product(): jnp.dot(left.T, right, precision=lax.Precision.HIGHEST, preferred_element...  38.1 us
    dot_general x2, matrix products, per_device(): jnp.dot(feats, weights, precision=lax.Precision.HIGHEST, preferred_elemen...  32.2 us
  transfers between devices with their start and end apart: 3, of which 3 were waited for; matrix products, arithmetic and copies ran while one was open for 7% of the time, Pallas kernels for 0%

commit v1 on v0

--- a/solution.py
+++ b/solution.py
@@ -47,7 +47,7 @@
         feats = feature_list[step_index]
         cross_local = local_product(feats, residual)
         gram_sum = grams_all[step_index]
-        cross_sum = lax.psum(cross_local, ("wide", "narrow"))
+        cross_sum = lax.psum(lax.psum(cross_local, "wide"), "narrow")
         weights = solve_block(gram_sum, cross_sum)
         residual = residual - jnp.dot(
             feats, weights, precision=lax.Precision.HIGHEST, preferred_element_type=jnp.float32

time: 871 us -> 941 us (1.080)
  waiting for transfers between devices: 332 us -> 394 us
    psum x2 -> x5, waiting for transfers between devices: 246 us -> 308 us  [the longest x4 178 us: per_device(): cross_sum = lax.psum(lax.psum(cross_local, 'wide'), 'narrow')]
  transfers between devices with their start and end apart: 3 -> 6, of which waited for: 3 -> 4; matrix products, arithmetic and copies ran while one was open for 7% -> 33% of each run, Pallas kernels for 0% -> 0%
where the time goes in v1:
time: 941 us; the launch traced here: 931 us
  waiting for transfers between devices  394 us (42%)
  other arithmetic  263 us (28%)
  matrix products  148 us (16%)
  blocking collectives  69.2 us (7%)
  local copies, waits for them, and re-layouts  33.6 us (4%)
  between operations  22.8 us (2%)
    psum x4, waiting for transfers between devices, per_device(): cross_sum = lax.psum(lax.psum(cross_local, 'wide'), 'narrow')  178 us
    another operation x30, other arithmetic, solve_block(): jnp.linalg.cholesky(gram_sum + damping * jnp.eye(width, dtype=gram_sum.dt...  160 us
    psum x1, waiting for transfers between devices, per_device(): grams_all = lax.psum(grams_local, ('wide', 'narrow'))  131 us
    psum x1, waiting for transfers between devices, from_root(): return lax.psum(kept, axis)  85.5 us
    another operation x5, other arithmetic, solve_block(): return jax.scipy.linalg.cho_solve((factor, True), cross_sum)  82.8 us
    psum x1, blocking collectives, from_root(): return lax.psum(kept, axis)  69.2 us
    another operation x28, matrix products, solve_block(): return jax.scipy.linalg.cho_solve((factor, True), cross_sum)  44.1 us
    dot_general x4, matrix products, local_product(): jnp.dot(left.T, right, precision=lax.Precision.HIGHEST, preferred_element...  39.8 us
  transfers between devices with their start and end apart: 6, of which 4 were waited for; matrix products, arithmetic and copies ran while one was open for 33% of the time, Pallas kernels for 0%

profile of v1, /device:TPU:1, one launch (start us, length us, event | category | flops | bytes accessed | tf_op | source)
XLA Modules:
  0.0 930.6 jit_solution(10149474691988061991)
XLA Ops:
  12.6 69.2 %all-reduce.1 = (f32[512]{0:T(512)S(1)}, f32[512]{0:T(512)S(1)}) all-reduce(f32[512]{0:T(512)S(1)} %bitcast.161, f32[512]{0:T(512)S(1)} %bitcast.160), channel_id=1, replica_groups=mesh['wide'=32,'narrow'=4] {'wide','narrow'}, use_global_device_ids=true, to_apply=%region_1.2 | all-reduce | flops 1024 | bytes 8192 | tf_op jit(solution)/shard_map/psum | solution.py:11
  81.8 85.5 %all-reduce.20.cloned.1.call-done = (f32[440,512]{1,0:T(8,128)}, f32[440,512]{1,0:T(8,128)}) async-done(((f32[440,512]{1,0:T(8,128)}, f32[440,512]{1,0:T(8,128)}), (f32[440,512]{1,0:T(8,128)}, f32[440,512]{1,0:T(8,128)})) %all-reduce.20.cloned.1.call-update) | async-done | bytes 1802256 | tf_op jit(solution)/shard_map/psum | solution.py:11
  167.3 11.2 %cosine_multiply_fusion.1 = f32[512,1024]{1,0:T(8,128)S(1)} fusion(f32[440,512]{1,0:T(8,128)} %get-tuple-element.40, f32[1024,440]{0,1:T(8,128)S(1)} %copy-done, f32[512]{0:T(512)S(1)} %get-tuple-element.38), kind=kOutput, calls=%fused_computation.61 | convolution fusion | flops 2769289216 | bytes 4802560 | tf_op jit(solution)/shard_map/dot_general | solution.py:15
  178.6 3.8 convolution_bitcast_fusion.1
  182.4 10.5 %cosine_multiply_fusion = f32[512,1024]{1,0:T(8,128)S(1)} fusion(f32[440,512]{1,0:T(8,128)S(1)} %copy-done.17, f32[1024,440]{0,1:T(8,128)S(1)} %copy-done, f32[512]{0:T(512)S(1)} %get-tuple-element.39), kind=kOutput, calls=%fused_computation.60 | convolution fusion | flops 2769289216 | bytes 4802560 | tf_op jit(solution)/shard_map/dot_general | solution.py:15
  200.2 17.3 %fusion.117 = f32[512,2048]{1,0:T(8,128)} fusion(f32[512,1024]{1,0:T(8,128)S(1)} %copy-done.6, f32[1024,2048]{1,0:T(8,128)} %param.9), kind=kOutput, calls=%fused_computation.198 | convolution fusion | flops 12884901888 | bytes 14680064 | tf_op jit(solution)/shard_map/dot_general | solution.py:22
  217.6 130.7 %all-reduce.10.cloned.1.call-done = f32[2,512,512]{1,2,0:T(8,128)} async-done(((f32[2,512,512]{1,2,0:T(8,128)}), f32[2,512,512]{1,2,0:T(8,128)}) %all-reduce.10.cloned.1.call-update) | async-done | bytes 2097168 | tf_op jit(solution)/shard_map/psum | solution.py:43
  358.8 11.7 %cholesky.286 = f32[128,128]{1,0:T(8,128)S(1)} custom-call(f32[128,128]{1,0:T(8,128)S(1)} %cholesky.426), custom_call_target="Cholesky" | custom-call | tf_op jit(solution)/shard_map/jit(cholesky)/cholesky | solution.py:30
  370.6 92.0 %all-reduce.12.cloned.1.call-done = f32[512,2048]{1,0:T(8,128)} async-done(((f32[512,2048]{1,0:T(8,128)}), f32[512,2048]{1,0:T(8,128)}) %all-reduce.12.cloned.1.call-update) | async-done | bytes 4194320 | tf_op jit(solution)/shard_map/psum | solution.py:50
  462.9 9.8 %custom-call.29 = f32[1,128,128]{1,2,0:T(8,128)S(1)} custom-call(f32[1,128,128]{2,1,0:T(8,128)S(1)} %get-tuple-element.69), custom_call_target="InvertDiagBlocksLowerTriangular" | custom-call | tf_op jit(solution)/shard_map/jit(cholesky)/cholesky | solution.py:30
  473.5 11.7 %cholesky.305 = f32[128,128]{1,0:T(8,128)S(1)} custom-call(f32[128,128]{1,0:T(8,128)S(1)} %cholesky.430), custom_call_target="Cholesky" | custom-call | tf_op jit(solution)/shard_map/jit(cholesky)/cholesky | solution.py:30
  485.2 9.8 %custom-call.30 = f32[1,128,128]{1,2,0:T(8,128)S(1)} custom-call(f32[1,128,128]{2,1,0:T(8,128)S(1)} %get-tuple-element.66), custom_call_target="InvertDiagBlocksLowerTriangular" | custom-call | tf_op jit(solution)/shard_map/jit(cholesky)/cholesky | solution.py:30
  495.7 11.9 %cholesky.326 = f32[128,128]{1,0:T(8,128)S(1)} custom-call(f32[128,128]{1,0:T(8,128)S(1)} %cholesky.435), custom_call_target="Cholesky" | custom-call | tf_op jit(solution)/shard_map/jit(cholesky)/cholesky | solution.py:30
  507.6 9.8 %custom-call.31 = f32[1,128,128]{1,2,0:T(8,128)S(1)} custom-call(f32[1,128,128]{2,1,0:T(8,128)S(1)} %get-tuple-element.63), custom_call_target="InvertDiagBlocksLowerTriangular" | custom-call | tf_op jit(solution)/shard_map/jit(cholesky)/cholesky | solution.py:30
  518.1 11.7 %cholesky.343 = f32[128,128]{1,0:T(8,128)S(1)} custom-call(f32[128,128]{1,0:T(8,128)S(1)} %convolution_subtract_fusion.15), custom_call_target="Cholesky" | custom-call | tf_op jit(solution)/shard_map/jit(cholesky)/cholesky | solution.py:30
  535.2 8.3 while.4
  543.6 39.8 %custom-call.32 = f32[4,128,128]{1,2,0:T(8,128)S(1)} custom-call(f32[4,128,128]{2,1,0:T(8,128)S(1)} %get-tuple-element.18), custom_call_target="InvertDiagBlocksLowerTriangular" | custom-call | tf_op jit(solution)/shard_map/jit(_cho_solve)/triangular_solve | solution.py:31
  608.0 16.1 %convolution_subtract_fusion.1 = f32[1024,2048]{1,0:T(8,128)S(1)} fusion(f32[1024,2048]{1,0:T(8,128)S(1)} %bitcast.159, f32[512,1024]{1,0:T(8,128)S(1)} %copy-done.7, f32[128,2048]{1,0:T(8,128)S(1)} %fusion.95, f32[128,2048]{1,0:T(8,128)} %copy-done.8, f32[128,2048]{1,0:T(8,128)} %copy-done.10, f32[128,2048]{1,0:T(8,128)} %fusion.90), kind=kOutput, calls=%fused_computation.8 | convolution fusion | flops 12890144768 | bytes 23068672 | tf_op jit(solution)/shard_map/dot_general | solution.py:52
  627.5 15.2 %fusion.118 = f32[512,2048]{1,0:T(8,128)} fusion(f32[512,1024]{1,0:T(8,128)S(1)} %copy-done.4, f32[1024,2048]{1,0:T(8,128)S(1)} %convolution_subtract_fusion.1), kind=kOutput, calls=%fused_computation.199 | convolution fusion | flops 12884901888 | bytes 14680064 | tf_op jit(solution)/shard_map/dot_general | solution.py:22
  644.0 11.7 %cholesky.358 = f32[128,128]{1,0:T(8,128)S(1)} custom-call(f32[128,128]{1,0:T(8,128)S(1)} %cholesky.439), custom_call_target="Cholesky" | custom-call | tf_op jit(solution)/shard_map/jit(cholesky)/cholesky | solution.py:30
  655.8 9.8 %custom-call.33 = f32[1,128,128]{1,2,0:T(8,128)S(1)} custom-call(f32[1,128,128]{2,1,0:T(8,128)S(1)} %get-tuple-element.59), custom_call_target="InvertDiagBlocksLowerTriangular" | custom-call | tf_op jit(solution)/shard_map/jit(cholesky)/cholesky | solution.py:30
  668.7 85.7 %all-reduce.16.cloned.1.call-done = f32[512,2048]{1,0:T(8,128)} async-done(((f32[512,2048]{1,0:T(8,128)}), f32[512,2048]{1,0:T(8,128)}) %all-reduce.16.cloned.1.call-update) | async-done | bytes 4194320 | tf_op jit(solution)/shard_map/psum | solution.py:50
  755.7 11.7 %cholesky.377 = f32[128,128]{1,0:T(8,128)S(1)} custom-call(f32[128,128]{1,0:T(8,128)S(1)} %cholesky.443), custom_call_target="Cholesky" | custom-call | tf_op jit(solution)/shard_map/jit(cholesky)/cholesky | solution.py:30
  768.1 10.0 %custom-call.34 = f32[1,128,128]{1,2,0:T(8,128)S(1)} custom-call(f32[1,128,128]{2,1,0:T(8,128)S(1)} %get-tuple-element.56), custom_call_target="InvertDiagBlocksLowerTriangular" | custom-call | tf_op jit(solution)/shard_map/jit(cholesky)/cholesky | solution.py:30
  780.4 11.7 %cholesky.398 = f32[128,128]{1,0:T(8,128)S(1)} custom-call(f32[128,128]{1,0:T(8,128)S(1)} %cholesky.448), custom_call_target="Cholesky" | custom-call | tf_op jit(solution)/shard_map/jit(cholesky)/cholesky | solution.py:30
  792.8 9.8 %custom-call.35 = f32[1,128,128]{1,2,0:T(8,128)S(1)} custom-call(f32[1,128,128]{2,1,0:T(8,128)S(1)} %get-tuple-element.53), custom_call_target="InvertDiagBlocksLowerTriangular" | custom-call | tf_op jit(solution)/shard_map/jit(cholesky)/cholesky | solution.py:30
  804.8 11.7 %cholesky.415 = f32[128,128]{1,0:T(8,128)S(1)} custom-call(f32[128,128]{1,0:T(8,128)S(1)} %convolution_subtract_fusion.14), custom_call_target="Cholesky" | custom-call | tf_op jit(solution)/shard_map/jit(cholesky)/cholesky | solution.py:30
  824.7 11.2 %while.5 = (s32[]{:T(128)}, f32[512,512]{1,0:T(8,128)}, s32[4,2]{0,1:T(2,128)S(1)}, f32[4,128,128]{2,1,0:T(8,128)S(1)}, s32[]{:T(128)}) while((s32[]{:T(128)}, f32[512,512]{1,0:T(8,128)}, s32[4,2]{0,1:T(2,128)S(1)}, f32[4,128,128]{2,1,0:T(8,128)S(1)}, s32[]{:T(128)}) %tuple.79), condition=%wide.while_cond.clone, body=%wide.while_body.clone.sunk | while | flops 2 | bytes 131189 | solution.py:31
  836.6 40.5 %custom-call.36 = f32[4,128,128]{1,2,0:T(8,128)S(1)} custom-call(f32[4,128,128]{2,1,0:T(8,128)} %copy-done.18), custom_call_target="InvertDiagBlocksLowerTriangular" | custom-call | tf_op jit(solution)/shard_map/jit(_cho_solve)/triangular_solve | solution.py:31
  877.2 4.3 fusion.37
  901.4 16.0 %convolution_subtract_fusion = f32[1024,2048]{1,0:T(8,128)} fusion(f32[1024,2048]{1,0:T(8,128)S(1)} %bitcast.157, f32[512,1024]{1,0:T(8,128)S(1)} %copy-done.4, f32[128,2048]{1,0:T(8,128)S(1)} %fusion.102, f32[128,2048]{1,0:T(8,128)S(1)} %fusion.100, f32[128,2048]{1,0:T(8,128)S(1)} %fusion.98, f32[128,2048]{1,0:T(8,128)S(1)} %fusion.97), kind=kOutput, calls=%fused_computation.7 | convolution fusion | flops 12890144768 | bytes 23068672 | tf_op jit(solution)/shard_map/dot_general | solution.py:52
  919.6 4.0 pad_maximum_fusion
  (169 shorter events, 113.0 us)
Async XLA Ops:
  7.2 160.2 %copy-start = (f32[1024,440]{0,1:T(8,128)S(1)}, f32[1024,440]{0,1:T(8,128)}, u32[]{:S(2)}) copy-start(f32[1024,440]{0,1:T(8,128)} %param.8) | copy-start | bytes 5406724
  7.2 5.4 copy-start.19
  7.2 160.1 %all-reduce.20.cloned.1.call-start = ((), (), s32[]{:S(2)}) async-start(), calls=%async_computation.5 | async-start | bytes 3604480 | tf_op jit(solution)/shard_map/psum | solution.py:11
  12.6 335.7 %all-reduce.10.cloned.1.call-start = ((), (), s32[]{:S(2)}) async-start(), calls=%async_computation | async-start | bytes 4194304 | tf_op jit(solution)/shard_map/psum | solution.py:43
  178.6 3.8 copy-start.5
  178.6 3.8 copy-start.17
  192.9 1.4 copy-start.3
  197.9 2.4 copy-start.6
  199.4 263.1 %all-reduce.12.cloned.1.call-start = ((), (), s32[]{:S(2)}) async-start(), calls=%async_computation.1 | async-start | bytes 8388608 | tf_op jit(solution)/shard_map/psum | solution.py:50
  217.5 365.8 %all-reduce.14.cloned.1.call-start = ((), (), s32[]{:S(2)}) async-start(), calls=%async_computation.2 | async-start | bytes 8388608 | tf_op jit(solution)/shard_map/psum | solution.py:50
  357.8 1.0 copy-start.15
  358.8 114.0 %copy-start.16 = (f32[512,512]{1,0:T(8,128)S(1)}, f32[512,512]{1,0:T(8,128)}, u32[]{:S(2)}) copy-start(f32[512,512]{1,0:T(8,128)} %copy-done.15) | copy-start | bytes 3145732
  462.6 291.8 %all-reduce.16.cloned.1.call-start = ((), (), s32[]{:S(2)}) async-start(), calls=%async_computation.3 | async-start | bytes 8388608 | tf_op jit(solution)/shard_map/psum | solution.py:50
  543.5 47.9 %copy-start.12 = (f32[512,512]{1,0:T(8,128)}, f32[512,512]{1,0:T(8,128)S(1)}, u32[]{:S(2)}) copy-start(f32[512,512]{1,0:T(8,128)S(1)} %get-tuple-element.185) | copy-start | bytes 3145732
  585.6 3.5 copy-start.13
  595.6 12.3 %slice-start.2 = ((s8[8388608]{0:T(1024)(128)(4,1)}), s8[4194304]{0:T(1024)(128)(4,1)S(1)}, s32[]{:S(2)}) async-start(s8[8388608]{0:T(1024)(128)(4,1)} %bitcast.158), calls=%async_computation.8 | async-start | bytes 8388608
  598.7 7.2 copy-start.8
  601.2 6.7 slice-start.3
  602.3 3.7 copy-start.10
  602.3 5.6 copy-start.7
  607.9 19.5 %copy-start.4 = (f32[512,1024]{1,0:T(8,128)S(1)}, f32[512,1024]{1,0:T(8,128)}, u32[]{:S(2)}) copy-start(f32[512,1024]{1,0:T(8,128)} %copy-done.3) | copy-start | bytes 6291460
  624.1 3.4 copy-start.2
  642.7 238.7 %all-reduce.18.cloned.1.call-start = ((), (), s32[]{:S(2)}) async-start(), calls=%async_computation.4 | async-start | bytes 8388608 | tf_op jit(solution)/shard_map/psum | solution.py:50
  835.9 0.7 copy-start.18
  883.7 3.5 copy-start.11
  883.7 3.5 copy-start.14
  894.8 6.6 slice-start
  897.3 4.1 slice-start.1
  917.4 2.2 copy-start.9
  919.6 4.0 copy-start.1
Sparse Core Ops, SparseCore 0:
  13.6 153.6 all-reduce.19
  199.5 148.6 all-reduce.9
  352.2 110.3 all-reduce.11
  464.8 92.4 all-reduce.13
  642.8 111.5 all-reduce.15
  756.7 92.4 all-reduce.17
